TPU v7x, 32 devices: a whole 2x2x4 slice. The times are simulated.
32 devices in a mesh: gx: 16 (over z, y, x), gy: 2 (over core).
Axes of the slice: x: 2, y: 2, z: 4, core: 2. Of those that a mesh axis runs over, the one named last changes fastest.
Arguments:
- density: float32 [128, 32, 64], P('gx', None, 'gy'), may hold values from 0.5 to 1.5
- momentum: float32 [3, 128, 32, 64], P(None, 'gx', None, 'gy'), may hold values from -3 to 3
- energy: float32 [128, 32, 64], P('gx', None, 'gy'), may hold values from 2.5 to 4
- eddy_normal_cell: int32 [1024], P('gx'), may hold values from 0 to 63
- eddy_spanwise_cell: int32 [1024], P('gx'), may hold values from 0 to 31
- eddy_signs: int32 [1024, 3], P('gx'), may hold values from 0 to 1
- eddy_strengths: float32 [1024], P('gx'), may hold values from 0.3 to 3
- filter_matrices: float32 [1, 128, 128], replicated, may hold values from -1.25 to 1.25
- shock_switch: int32 [1, 64], P(None, 'gy'), may hold values 0 or 1
- dilatation_bin: int32 [128, 32, 64], P('gx', None, 'gy'), may hold values from 0 to 63
- vorticity_bin: int32 [128, 32, 64], P('gx', None, 'gy'), may hold values from 0 to 63, as said below
Outputs:
- conserved_next: float32 [5, 128, 32, 64], P(None, 'gx', None, 'gy')
- histogram: float32 [64, 64], replicated
Inputs may be any that keep to these rules, and one draw needn't show every extreme that they name: vorticity_bin at streamwise cell x is x * 64 // 128 or one more, modulo 64.
All inputs are finite; a program needn't handle non-finite values. No bound on the sum of `shock_switch` on one device may be relied on, other than what follows from the above.
Results may differ from a plain program's by a relative error of at most 0.0003.
Values sent between devices are 32-bit elements; how exact they have to be, the bound alone decides.
No kernel may reach another device: no remote copies, remote signals or barrier semaphores. Data moves between devices by JAX's collectives and lax.ppermute only.
A program may use at most 64 MiB of HBM per device.

v0:
```python
import math
import jax
import jax.numpy as jnp
from jax import lax
from jax.sharding import PartitionSpec as P

HISTOGRAM_BINS = 64
SIGMA_Y = 32
SIGMA_Z = 8
TIME_STEP = 0.1
GAMMA_GAS = 1.4
SENSOR_EPS = 0.1
HAT_PEAK = math.sqrt(1.5)


def extended(x, sides, width):
    for axis, dim in sides:
        size, length = (lax.axis_size(axis), x.shape[dim])
        up = [(i, (i + 1) % size) for i in range(size - 1)]
        down = [(j, i) for i, j in up]
        last = lax.slice_in_dim(x, length - width, length, axis=dim)
        first = lax.slice_in_dim(x, 0, width, axis=dim)
        before = lax.ppermute(last, axis, up)
        after = lax.ppermute(first, axis, down)
        x = jnp.concatenate([before, x, after], axis=dim)
    return x


def hat_shape(centres, coords, spread, period):
    offset = coords[None, :] - centres[:, None]
    if period > 0:
        offset = jnp.mod(offset + period / 2, period) - period / 2
    return HAT_PEAK * jnp.maximum(0.0, 1.0 - jnp.abs(offset) / spread)


def inflow_from(centre_y, centre_z, eddy_weight, coords_y, coords_z, span):
    shape_y = hat_shape(centre_y, coords_y, float(SIGMA_Y), 0)
    shape_z = hat_shape(centre_z, coords_z, float(SIGMA_Z), span)
    weighted = (eddy_weight[:, :, None] * shape_z[:, None, :]).reshape(eddy_weight.shape[0], -1)
    inflow = jnp.dot(weighted.T, shape_y, precision=lax.Precision.HIGHEST)
    return inflow.reshape(3, coords_z.shape[0], coords_y.shape[0])


def ghost_state(inflow):
    mom_x = 1.0 + inflow[0]
    kinetic = mom_x * mom_x + inflow[1] * inflow[1] + inflow[2] * inflow[2]
    return jnp.stack([jnp.ones_like(mom_x), mom_x, inflow[1], inflow[2], 3.0 + 0.5 * kinetic])


def flux_of(fields, velocity, pressure, direction):
    result = fields * velocity[direction][None]
    result = result.at[1 + direction].add(pressure)
    return result.at[4].add(pressure * velocity[direction])


def central_x(values):
    return (values[..., 2:, :, 1:-1] - values[..., :-2, :, 1:-1]) * 0.5


def central_y(values):
    return (values[..., 1:-1, :, 2:] - values[..., 1:-1, :, :-2]) * 0.5


def central_z(values):
    centre = values[..., 1:-1, :, 1:-1]
    return (jnp.roll(centre, -1, axis=-2) - jnp.roll(centre, 1, axis=-2)) * 0.5


def section_rhs(padded):
    velocity = padded[1:4] / padded[0][None]
    pressure = (GAMMA_GAS - 1.0) * (padded[4] - 0.5 * jnp.sum(padded[1:4] * velocity, axis=0))
    change = central_x(flux_of(padded, velocity, pressure, 0))
    change = change + central_y(flux_of(padded, velocity, pressure, 1))
    change = change + central_z(flux_of(padded, velocity, pressure, 2))
    updated = padded[:, 1:-1, :, 1:-1] - TIME_STEP * change
    dilatation = central_x(velocity[0]) + central_y(velocity[1]) + central_z(velocity[2])
    vort_x = central_y(velocity[2]) - central_z(velocity[1])
    vort_y = central_z(velocity[0]) - central_x(velocity[2])
    vort_z = central_x(velocity[1]) - central_y(velocity[0])
    squared = dilatation * dilatation
    shock_sensor = squared / (
        squared + vort_x * vort_x + vort_y * vort_y + vort_z * vort_z + SENSOR_EPS
    )
    return (updated, shock_sensor)


def filter_lines(pencil, filter_matrices):
    block_count, block_len = (filter_matrices.shape[0], filter_matrices.shape[1])
    lanes = pencil.shape[2]
    blocks = pencil.reshape(5, block_count, block_len, lanes)
    smooth = jnp.einsum("bij,fbjp->fbip", filter_matrices, blocks, precision=lax.Precision.HIGHEST)
    return smooth.reshape(5, block_count * block_len, lanes)


def plane_histogram(shock_sensor, dilatation_bin, vorticity_bin):
    bin_levels = jnp.arange(HISTOGRAM_BINS, dtype=jnp.int32)

    def accumulate_plane(histogram_totals, histogram_parts):
        sensor_plane, plane_dilatation, plane_vorticity = histogram_parts
        flat_sensor = sensor_plane.reshape(-1)
        dilatation_table = (plane_dilatation.reshape(-1)[None, :] == bin_levels[:, None]).astype(
            jnp.float32
        )
        vorticity_table = jnp.where(
            plane_vorticity.reshape(-1)[:, None] == bin_levels[None, :], flat_sensor[:, None], 0.0
        )
        return (
            histogram_totals
            + jnp.dot(dilatation_table, vorticity_table, precision=lax.Precision.HIGHEST),
            None,
        )

    histogram_totals, _ = lax.scan(
        accumulate_plane,
        jnp.zeros((HISTOGRAM_BINS, HISTOGRAM_BINS), jnp.float32),
        (shock_sensor, dilatation_bin, vorticity_bin),
    )
    return histogram_totals


def shards(
    density,
    momentum,
    energy,
    eddy_normal_cell,
    eddy_spanwise_cell,
    eddy_signs,
    eddy_strengths,
    filter_matrices,
    shock_switch,
    dilatation_bin,
    vorticity_bin,
):
    cells_x, span, cells_y = density.shape
    slab_index = lax.axis_index("gx")
    block_index = lax.axis_index("gy")
    slab_count = lax.axis_size("gx")
    fields = jnp.concatenate([density[None], momentum, energy[None]], axis=0)
    total_y = cells_y * lax.axis_size("gy")
    total_eddies = eddy_normal_cell.shape[0] * slab_count
    amplitude = math.sqrt(total_y * span / (total_eddies * SIGMA_Y * SIGMA_Z))
    eddy_weight = (2 * eddy_signs - 1).astype(jnp.float32) * eddy_strengths[:, None] * amplitude
    coords_y = (block_index * cells_y + jnp.arange(cells_y, dtype=jnp.int32)).astype(jnp.float32)
    coords_z = jnp.arange(span, dtype=jnp.int32).astype(jnp.float32)
    partial_sum = inflow_from(
        eddy_normal_cell.astype(jnp.float32),
        eddy_spanwise_cell.astype(jnp.float32),
        eddy_weight,
        coords_y,
        coords_z,
        span,
    )
    inflow = lax.psum(partial_sum, "gx")
    ghost_cells = ghost_state(inflow)
    padded = extended(fields, (("gx", 1), ("gy", 3)), 1)
    padded = padded.at[:, 0, :, 1:-1].set(
        jnp.where(slab_index == 0, ghost_cells, padded[:, 0, :, 1:-1])
    )
    padded = padded.at[:, -1, :, 1:-1].set(
        jnp.where(slab_index == slab_count - 1, fields[:, -1], padded[:, -1, :, 1:-1])
    )
    padded = padded.at[:, 1:-1, :, 0].set(
        jnp.where(block_index == 0, fields[:, :, :, 0], padded[:, 1:-1, :, 0])
    )
    padded = padded.at[:, 1:-1, :, -1].set(
        jnp.where(
            block_index == lax.axis_size("gy") - 1, fields[:, :, :, -1], padded[:, 1:-1, :, -1]
        )
    )
    updated, shock_sensor = section_rhs(padded)
    block_len = filter_matrices.shape[1]
    filter_row = slab_index * cells_x // block_len
    mask_row = lax.dynamic_slice_in_dim(shock_switch, filter_row, 1, 0).astype(jnp.float32)
    weight = mask_row[None] * shock_sensor
    columns = span * cells_y
    stacked = updated.reshape(5, cells_x, columns)
    weight_flat = weight.reshape(1, cells_x, columns)
    pencil, pencil_weight = (
        lax.all_to_all(stacked, "gx", split_axis=2, concat_axis=1, tiled=True),
        lax.all_to_all(weight_flat, "gx", split_axis=2, concat_axis=1, tiled=True),
    )
    smooth = filter_lines(pencil, filter_matrices)
    returned = pencil + pencil_weight * (smooth - pencil)
    back_lines = lax.all_to_all(returned, "gx", split_axis=1, concat_axis=2, tiled=True)
    conserved_next = back_lines.reshape(5, cells_x, span, cells_y)
    partial_histogram = plane_histogram(shock_sensor, dilatation_bin, vorticity_bin)
    summed = lax.psum(partial_histogram, ("gx", "gy"))
    all_cells = cells_x * slab_count * span * total_y
    histogram = summed * (HISTOGRAM_BINS * HISTOGRAM_BINS / all_cells)
    return (conserved_next, histogram)


def solution(mesh):
    in_specs = (
        P("gx", None, "gy"),
        P(None, "gx", None, "gy"),
        P("gx", None, "gy"),
        P("gx"),
        P("gx"),
        P("gx", None),
        P("gx"),
        P(),
        P(None, "gy"),
        P("gx", None, "gy"),
        P("gx", None, "gy"),
    )
    out_specs = (P(None, "gx", None, "gy"), P())
    return jax.shard_map(shards, mesh=mesh, in_specs=in_specs, out_specs=out_specs, check_vma=False)
```

profile of v0, /device:TPU:0, one launch (start us, length us, event | category | flops | bytes accessed | tf_op | source)
XLA Modules:
  0.0 215.9 jit_solution(9551707045615207745)
XLA Ops:
  1.6 1.3 collective-permute-start.1
  2.9 5.5 %collective-permute-start = (f32[5,1,32,32]{3,2,0,1:T(8,128)S(1)}, f32[5,1,32,32]{3,2,0,1:T(8,128)S(1)}, u32[]{:S(2)}, u32[]{:S(2)}) collective-permute-start(f32[5,1,32,32]{3,2,0,1:T(8,128)S(1)} %get-tuple-element.222), channel_id=1, source_target_pairs={{0,2},{2,4},{4,6},{6,8},{8,10},{10,12},{12,14},{14,16},{16,18},{18... | collective-permute-start | bytes 61448 | tf_op jit(solution)/shard_map/ppermute | solution.py:23
  10.8 75.6 %psum.14 = f32[3,32,32]{2,1,0:T(8,128)S(1)} all-reduce(f32[3,32,32]{2,1,0:T(8,128)S(1)} %fusion.50), channel_id=1, replica_groups=mesh['gx'=16,'gy'=2] {'gx'}, use_global_device_ids=true, to_apply=%region_1.2 | all-reduce | flops 3072 | bytes 24576 | tf_op jit(solution)/shard_map/psum | solution.py:153
  91.2 1.3 collective-permute-start.3
  92.5 3.0 %collective-permute-start.2 = (f32[5,10,32,1]{2,3,1,0:T(1,128)S(1)}, f32[5,10,32,1]{2,3,1,0:T(1,128)S(1)}, u32[]{:S(2)}, u32[]{:S(2)}) collective-permute-start(f32[5,10,32,1]{2,3,1,0:T(1,128)S(1)} %copy.81), channel_id=1, source_target_pairs={{0,1},{2,3},{4,5},{6,7},{8,9},{10,11},{12,13},{14,15},{16,17},{18,... | collective-permute-start | bytes 19208 | tf_op jit(solution)/shard_map/ppermute | solution.py:23
  95.5 1.4 and_reduce_fusion
  97.3 1.3 copy.84
  98.6 1.6 pad_maximum_fusion.1
  100.2 1.4 fusion.48
  101.6 1.7 scatter.14
  105.9 3.7 %scatter.19 = f32[5,10,32,34]{3,2,0,1:T(8,128)S(1)} dynamic-update-slice(f32[5,10,32,34]{3,2,0,1:T(8,128)S(1)} %scatter.16, f32[5,8,32,1]{3,2,0,1:T(8,128)S(1)} %slice_select_fusion, s32[]{:T(128)} %constant.328.clone.1, s32[]{:T(128)} %constant.350.clone.1, s32[]{:T(128)} %constant.328.clone.1, s32[]{:T(128)} %constant.351.clone.1) | dynamic-update-slice | bytes 10244 | tf_op jit(solution)/shard_map/scatter | solution.py:165
  114.4 3.7 %reduce.27 = f32[1024,8]{1,0:T(8,128)} reduce(f32[1024,1,8]{2,1,0:T(1,128)} %bitcast.128, f32[]{:T(128)} %broadcast.273), dimensions={1}, to_apply=%bitcast.110.reduce_sub_computation | reduce | bytes 65540
  118.1 1.9 reshape.467
  120.0 3.5 %all-to-all-start.1 = ((f32[16,1,512]{2,1,0:T(1,128)}), f32[16,1,512]{2,1,0:T(1,128)S(1)}, u32[]{:S(2)}, u32[]{:S(2)}) async-start(f32[16,1,512]{2,1,0:T(1,128)} %reshape.467), calls=%async_computation.1 | async-start | bytes 65536 | tf_op jit(solution)/shard_map/all_to_all | solution.py:180
  123.5 2.7 %fusion.14 = f32[5,8,32,32]{3,2,0,1:T(8,128)} fusion(f32[5,10,32,34]{3,2,0,1:T(8,128)S(1)} %get-tuple-element.221, f32[5,10,32,34]{3,2,0,1:T(8,128)S(1)} %scatter.19, f32[5,8,1,32]{3,2,0,1:T(1,128)S(1)} %get-tuple-element.213, f32[5,8,31,32]{3,2,0,1:T(8,128)} %get-tuple-element.215, f32[5,8,31,32]{3,2,0,1:T(8,128)S(1)} %get-tuple-element.214, ...), kind=kLoop, calls=%fused_computation.23 | loop fusion | flops 368640 | bytes 4295680 | tf_op jit(solution)/shard_map/sub | solution.py:75
  126.2 3.6 %copy.122 = f32[5,8,32,32]{1,0,3,2:T(8,128)} copy(f32[5,8,32,32]{3,2,0,1:T(8,128)} %fusion.14) | data formatting | bytes 327680 | tf_op jit(solution)/shard_map/reshape | solution.py:176
  129.8 3.4 %reshape.465 = f32[16,1,2560]{2,1,0:T(1,128)} reshape(f32[1024,5,8]{2,1,0:T(8,128)} %bitcast.117) | data formatting | bytes 327680
  133.1 6.9 %all-to-all-start = ((f32[16,1,2560]{2,1,0:T(1,128)}), f32[16,1,2560]{2,1,0:T(1,128)S(1)}, u32[]{:S(2)}, u32[]{:S(2)}) async-start(f32[16,1,2560]{2,1,0:T(1,128)} %reshape.465), calls=%async_computation | async-start | bytes 327680 | tf_op jit(solution)/shard_map/all_to_all | solution.py:179
  141.8 6.1 %all-to-all-done = f32[16,1,2560]{2,1,0:T(1,128)S(1)} async-done(((f32[16,1,2560]{2,1,0:T(1,128)}), f32[16,1,2560]{2,1,0:T(1,128)S(1)}, u32[]{:S(2)}, u32[]{:S(2)}) %all-to-all-start) | async-done | bytes 163872 | tf_op jit(solution)/shard_map/all_to_all | solution.py:179
  148.9 2.6 %reshape.466 = f32[1024,5,8]{2,1,0:T(8,128)} reshape(f32[16,2560]{1,0:T(8,128)S(1)} %reduce.26) | data formatting | bytes 327680
  151.5 2.6 %copy.103 = f32[5,16,8,64]{3,2,1,0:T(8,128)S(1)} copy(f32[5,16,8,64]{2,0,3,1:T(8,128)} %bitcast.118) | data formatting | bytes 327680 | tf_op jit(solution)/shard_map/all_to_all | solution.py:179
  156.1 3.5 %all-to-all-start.2 = ((f32[16,1,2560]{2,1,0:T(1,128)}), f32[16,1,2560]{2,1,0:T(1,128)S(1)}, u32[]{:S(2)}, u32[]{:S(2)}) async-start(f32[16,1,2560]{2,1,0:T(1,128)} %reshape.469), calls=%async_computation.2 | async-start | bytes 327680 | tf_op jit(solution)/shard_map/all_to_all | solution.py:184
  159.6 12.6 %while.22 = (s32[]{:T(128)}, f32[64,64]{1,0:T(8,128)S(1)}, s32[8,32,32]{2,1,0:T(8,128)}, s32[8,32,32]{2,1,0:T(8,128)}, f32[8,32,32]{2,1,0:T(8,128)S(1)}, /*index=5*/s32[]{:T(128)}, s32[]{:T(128)}) while((s32[]{:T(128)}, f32[64,64]{1,0:T(8,128)S(1)}, s32[8,32,32]{2,1,0:T(8,128)}, s32[8,32,32]{2,1,0:T(8,128)}, ...), condition=%wide.region_4.5_spmd.clone.clone, body=%wide.region_3.4_spmd.clone.clone.sunk | while | flops 50536448 | bytes 94311 | solution.py:113
  172.2 40.8 %psum.15 = f32[64,64]{1,0:T(8,128)S(1)} all-reduce(f32[64,64]{1,0:T(8,128)S(1)} %get-tuple-element.157), channel_id=1, replica_groups=mesh['gx'=16,'gy'=2] {'gx','gy'}, use_global_device_ids=true, to_apply=%region_5.6 | all-reduce | flops 4096 | bytes 32768 | tf_op jit(solution)/shard_map/psum | solution.py:187
  (125 shorter events, 35.6 us)
Async XLA Ops:
  0.6 153.6 %copy-start = (f32[1,128,128]{2,1,0:T(8,128)S(1)}, f32[1,128,128]{2,1,0:T(8,128)}, u32[]{:S(2)}) copy-start(f32[1,128,128]{2,1,0:T(8,128)} %param.40) | copy-start | bytes 196612
  1.6 93.9 %copy-start.4 = (s32[4]{0:T(128)S(1)}, s32[4]{0:T(128)}, u32[]{:S(2)}) copy-start(s32[4]{0:T(128)} %constant.330.clone.1) | copy-start | bytes 52
  1.6 87.3 %collective-permute-start.1 = (f32[5,1,32,32]{3,2,0,1:T(8,128)S(1)}, f32[5,1,32,32]{3,2,0,1:T(8,128)S(1)}, u32[]{:S(2)}, u32[]{:S(2)}) collective-permute-start(f32[5,1,32,32]{3,2,0,1:T(8,128)S(1)} %get-tuple-element.223), channel_id=1, source_target_pairs={{2,0},{4,2},{6,4},{8,6},{10,8},{12,10},{14,12},{16,14},{18,16},{20... | collective-permute-start | bytes 61448 | tf_op jit(solution)/shard_map/ppermute | solution.py:24
  2.9 86.0 %collective-permute-start = (f32[5,1,32,32]{3,2,0,1:T(8,128)S(1)}, f32[5,1,32,32]{3,2,0,1:T(8,128)S(1)}, u32[]{:S(2)}, u32[]{:S(2)}) collective-permute-start(f32[5,1,32,32]{3,2,0,1:T(8,128)S(1)} %get-tuple-element.222), channel_id=1, source_target_pairs={{0,2},{2,4},{4,6},{6,8},{8,10},{10,12},{12,14},{14,16},{16,18},{18... | collective-permute-start | bytes 61448 | tf_op jit(solution)/shard_map/ppermute | solution.py:23
  87.6 11.0 %copy-start.1 = (f32[3,8,32,32]{3,2,1,0:T(8,128)S(1)}, f32[3,8,32,32]{3,2,1,0:T(8,128)}, u32[]{:S(2)}) copy-start(f32[3,8,32,32]{3,2,1,0:T(8,128)} %param.34) | copy-start | bytes 294916
  87.6 11.0 %copy-start.2 = (f32[8,32,32]{2,1,0:T(8,128)S(1)}, f32[8,32,32]{2,1,0:T(8,128)}, u32[]{:S(2)}) copy-start(f32[8,32,32]{2,1,0:T(8,128)} %param.35) | copy-start | bytes 98308
  87.6 11.0 %copy-start.3 = (f32[8,32,32]{2,1,0:T(8,128)S(1)}, f32[8,32,32]{2,1,0:T(8,128)}, u32[]{:S(2)}) copy-start(f32[8,32,32]{2,1,0:T(8,128)} %param.33) | copy-start | bytes 98308
  91.2 6.1 %collective-permute-start.3 = (f32[5,10,32,1]{2,3,1,0:T(1,128)S(1)}, f32[5,10,32,1]{2,3,1,0:T(1,128)S(1)}, u32[]{:S(2)}, u32[]{:S(2)}) collective-permute-start(f32[5,10,32,1]{2,3,1,0:T(1,128)S(1)} %copy.82), channel_id=1, source_target_pairs={{1,0},{3,2},{5,4},{7,6},{9,8},{11,10},{13,12},{15,14},{17,16},{19,... | collective-permute-start | bytes 19208 | tf_op jit(solution)/shard_map/ppermute | solution.py:24
  92.5 4.4 %collective-permute-start.2 = (f32[5,10,32,1]{2,3,1,0:T(1,128)S(1)}, f32[5,10,32,1]{2,3,1,0:T(1,128)S(1)}, u32[]{:S(2)}, u32[]{:S(2)}) collective-permute-start(f32[5,10,32,1]{2,3,1,0:T(1,128)S(1)} %copy.81), channel_id=1, source_target_pairs={{0,1},{2,3},{4,5},{6,7},{8,9},{10,11},{12,13},{14,15},{16,17},{18,... | collective-permute-start | bytes 19208 | tf_op jit(solution)/shard_map/ppermute | solution.py:23
  120.0 13.2 %all-to-all-start.1 = ((f32[16,1,512]{2,1,0:T(1,128)}), f32[16,1,512]{2,1,0:T(1,128)S(1)}, u32[]{:S(2)}, u32[]{:S(2)}) async-start(f32[16,1,512]{2,1,0:T(1,128)} %reshape.467), calls=%async_computation.1 | async-start | bytes 65536 | tf_op jit(solution)/shard_map/all_to_all | solution.py:180
  133.1 14.8 %all-to-all-start = ((f32[16,1,2560]{2,1,0:T(1,128)}), f32[16,1,2560]{2,1,0:T(1,128)S(1)}, u32[]{:S(2)}, u32[]{:S(2)}) async-start(f32[16,1,2560]{2,1,0:T(1,128)} %reshape.465), calls=%async_computation | async-start | bytes 327680 | tf_op jit(solution)/shard_map/all_to_all | solution.py:179
  156.1 57.5 %all-to-all-start.2 = ((f32[16,1,2560]{2,1,0:T(1,128)}), f32[16,1,2560]{2,1,0:T(1,128)S(1)}, u32[]{:S(2)}, u32[]{:S(2)}) async-start(f32[16,1,2560]{2,1,0:T(1,128)} %reshape.469), calls=%async_computation.2 | async-start | bytes 327680 | tf_op jit(solution)/shard_map/all_to_all | solution.py:184
where the time goes:
time: 218 us; the launch traced here: 216 us
  blocking collectives  116 us (53%)
  local copies, waits for them, and re-layouts  39.7 us (18%)
  starting transfers between devices  25 us (11%)
  other arithmetic  21.8 us (10%)
  waiting for transfers between devices  6.13 us (3%)
  matrix products  5.55 us (3%)
    psum x1, blocking collectives, shards(): inflow = lax.psum(partial_sum, 'gx')  75.6 us
    psum x1, blocking collectives, shards(): summed = lax.psum(partial_histogram, ('gx', 'gy'))  40.8 us
    unnamed x16, local copies, waits for them, and re-layouts  9.82 us
    ppermute x2, starting transfers between devices, extended(): before = lax.ppermute(last, axis, up)  8.5 us
    all_to_all x1, starting transfers between devices, shards(): lax.all_to_all(stacked, 'gx', split_axis=2, concat_axis=1, tiled=True)  6.88 us
    all_to_all x1, waiting for transfers between devices, shards(): lax.all_to_all(stacked, 'gx', split_axis=2, concat_axis=1, tiled=True)  6.11 us
    dynamic_slice x16, local copies, waits for them, and re-layouts, plane_histogram(): lax.scan(accumulate_plane, jnp.zeros((HISTOGRAM_BINS, HISTOGRAM_BINS), jn...  6 us
    dot_general x8, matrix products, accumulate_plane(): jnp.dot(dilatation_table, vorticity_table, precision=lax.Precision.HIGHEST)  4.61 us
  transfers between devices with their start and end apart: 7, of which 1 were waited for; matrix products, arithmetic and copies ran while one was open for 14% of the time, Pallas kernels for 0%

commit v1 on v0

--- a/solution.py
+++ b/solution.py
@@ -176,7 +176,10 @@
     stacked = updated.reshape(5, cells_x, columns)
     weight_flat = weight.reshape(1, cells_x, columns)
     pencil, pencil_weight = (
-        lax.all_to_all(stacked, "gx", split_axis=2, concat_axis=1, tiled=True),
+        jnp.concatenate(
+            lax.all_to_all(jnp.stack(jnp.split(stacked, lax.axis_size("gx"), axis=2)), "gx", 0, 0),
+            axis=1,
+        ),
         lax.all_to_all(weight_flat, "gx", split_axis=2, concat_axis=1, tiled=True),
     )
     smooth = filter_lines(pencil, filter_matrices)

time: 218 us -> 207 us (0.950)
  local copies, waits for them, and re-layouts: 39.7 us -> 32.8 us
  other arithmetic: 21.8 us -> 17.2 us
    all_to_all x3 -> x1, local copies, waits for them, and re-layouts: 3.26 us -> 0.54 us  [shards(): lax.all_to_all(jnp.stack(jnp.split(stacked, lax.axis_size('gx'), axis=2))...]
    unnamed x16 -> x41, local copies, waits for them, and re-layouts: 9.82 us -> 7.49 us
    reshape x1, local copies, waits for them, and re-layouts: 3.59 us -> 1.4 us  [shards(): stacked = updated.reshape(5, cells_x, columns)]
  transfers between devices with their start and end apart: 7 -> 7, of which waited for: 1 -> 2; matrix products, arithmetic and copies ran while one was open for 14% -> 11% of each run, Pallas kernels for 0% -> 0%
where the time goes in v1:
time: 207 us; the launch traced here: 205 us
  blocking collectives  116 us (56%)
  local copies, waits for them, and re-layouts  32.8 us (16%)
  starting transfers between devices  22.9 us (11%)
  other arithmetic  17.2 us (8%)
  waiting for transfers between devices  8.1 us (4%)
  matrix products  5.55 us (3%)
    psum x1, blocking collectives, shards(): inflow = lax.psum(partial_sum, 'gx')  75.7 us
    psum x1, blocking collectives, shards(): summed = lax.psum(partial_histogram, ('gx', 'gy'))  40.8 us
    ppermute x2, starting transfers between devices, extended(): before = lax.ppermute(last, axis, up)  8.5 us
    unnamed x41, local copies, waits for them, and re-layouts  7.49 us
    all_to_all x1, waiting for transfers between devices, shards(): lax.all_to_all(jnp.stack(jnp.split(stacked, lax.axis_size('gx'), axis=2))...  6.04 us
    dynamic_slice x16, local copies, waits for them, and re-layouts, plane_histogram(): lax.scan(accumulate_plane, jnp.zeros((HISTOGRAM_BINS, HISTOGRAM_BINS), jn...  6 us
    all_to_all x1, starting transfers between devices, shards(): lax.all_to_all(jnp.stack(jnp.split(stacked, lax.axis_size('gx'), axis=2))...  4.84 us
    dot_general x8, matrix products, accumulate_plane(): jnp.dot(dilatation_table, vorticity_table, precision=lax.Precision.HIGHEST)  4.61 us
  transfers between devices with their start and end apart: 7, of which 2 were waited for; matrix products, arithmetic and copies ran while one was open for 11% of the time, Pallas kernels for 0%

profile of v1, /device:TPU:0, one launch (start us, length us, event | category | flops | bytes accessed | tf_op | source)
XLA Modules:
  0.0 204.6 jit_solution(10315833878143292865)
XLA Ops:
  1.6 1.3 collective-permute-start.1
  2.9 5.5 %collective-permute-start = (f32[5,1,32,32]{3,2,0,1:T(8,128)S(1)}, f32[5,1,32,32]{3,2,0,1:T(8,128)S(1)}, u32[]{:S(2)}, u32[]{:S(2)}) collective-permute-start(f32[5,1,32,32]{3,2,0,1:T(8,128)S(1)} %get-tuple-element.222), channel_id=1, source_target_pairs={{0,2},{2,4},{4,6},{6,8},{8,10},{10,12},{12,14},{14,16},{16,18},{18... | collective-permute-start | bytes 61448 | tf_op jit(solution)/shard_map/ppermute | solution.py:23
  10.2 75.7 %psum.14 = f32[3,32,32]{2,1,0:T(8,128)S(1)} all-reduce(f32[3,32,32]{2,1,0:T(8,128)S(1)} %fusion.50), channel_id=1, replica_groups=mesh['gx'=16,'gy'=2] {'gx'}, use_global_device_ids=true, to_apply=%region_1.2 | all-reduce | flops 3072 | bytes 24576 | tf_op jit(solution)/shard_map/psum | solution.py:153
  88.3 1.3 collective-permute-start.3
  89.6 3.0 %collective-permute-start.2 = (f32[5,10,32,1]{2,3,1,0:T(1,128)S(1)}, f32[5,10,32,1]{2,3,1,0:T(1,128)S(1)}, u32[]{:S(2)}, u32[]{:S(2)}) collective-permute-start(f32[5,10,32,1]{2,3,1,0:T(1,128)S(1)} %copy.81), channel_id=1, source_target_pairs={{0,1},{2,3},{4,5},{6,7},{8,9},{10,11},{12,13},{14,15},{16,17},{18,... | collective-permute-start | bytes 19208 | tf_op jit(solution)/shard_map/ppermute | solution.py:23
  93.3 1.4 and_reduce_fusion
  95.1 1.3 copy.84
  96.3 1.6 pad_maximum_fusion.1
  98.0 1.4 fusion.48
  99.4 1.7 scatter.14
  103.6 3.7 %scatter.19 = f32[5,10,32,34]{3,2,0,1:T(8,128)S(1)} dynamic-update-slice(f32[5,10,32,34]{3,2,0,1:T(8,128)S(1)} %scatter.16, f32[5,8,32,1]{3,2,0,1:T(8,128)S(1)} %slice_select_fusion, s32[]{:T(128)} %constant.328.clone.1, s32[]{:T(128)} %constant.350.clone.1, s32[]{:T(128)} %constant.328.clone.1, s32[]{:T(128)} %constant.351.clone.1) | dynamic-update-slice | bytes 10244 | tf_op jit(solution)/shard_map/scatter | solution.py:165
  109.0 1.2 fusion.90
  110.6 1.0 copy.114
  112.2 3.8 %reduce.27 = f32[1024,8]{1,0:T(8,128)} reduce(f32[1024,1,8]{2,1,0:T(1,128)} %bitcast.192, f32[]{:T(128)} %broadcast.273), dimensions={1}, to_apply=%bitcast.172.reduce_sub_computation | reduce | bytes 65540
  115.9 1.9 reshape.473
  117.9 3.5 %all-to-all-start.1 = ((f32[16,1,512]{2,1,0:T(1,128)}), f32[16,1,512]{2,1,0:T(1,128)S(1)}, u32[]{:S(2)}, u32[]{:S(2)}) async-start(f32[16,1,512]{2,1,0:T(1,128)} %reshape.473), calls=%async_computation.1 | async-start | bytes 65536 | tf_op jit(solution)/shard_map/all_to_all | solution.py:183
  121.4 2.7 %fusion.14 = f32[5,8,32,32]{3,2,0,1:T(8,128)} fusion(f32[5,10,32,34]{3,2,0,1:T(8,128)S(1)} %get-tuple-element.221, f32[5,10,32,34]{3,2,0,1:T(8,128)S(1)} %scatter.19, f32[5,8,1,32]{3,2,0,1:T(1,128)S(1)} %get-tuple-element.213, f32[5,8,31,32]{3,2,0,1:T(8,128)} %get-tuple-element.215, f32[5,8,31,32]{3,2,0,1:T(8,128)S(1)} %get-tuple-element.214, ...), kind=kLoop, calls=%fused_computation.23 | loop fusion | flops 368640 | bytes 4295680 | tf_op jit(solution)/shard_map/sub | solution.py:75
  124.1 1.4 reshape.469
  126.7 2.0 all-to-all-done.1
  128.7 4.8 %all-to-all-start = ((f32[16,1,2560]{2,1,0:T(1,128)}), f32[16,1,2560]{2,1,0:T(1,128)S(1)}, u32[]{:S(2)}, u32[]{:S(2)}) async-start(f32[16,1,2560]{2,1,0:T(1,128)} %reshape.471), calls=%async_computation | async-start | bytes 327680 | tf_op jit(solution)/shard_map/all_to_all | solution.py:180
  135.5 6.0 %all-to-all-done = f32[16,1,2560]{2,1,0:T(1,128)S(1)} async-done(((f32[16,1,2560]{2,1,0:T(1,128)}), f32[16,1,2560]{2,1,0:T(1,128)S(1)}, u32[]{:S(2)}, u32[]{:S(2)}) %all-to-all-start) | async-done | bytes 163872 | tf_op jit(solution)/shard_map/all_to_all | solution.py:180
  144.7 3.5 %all-to-all-start.2 = ((f32[16,1,2560]{2,1,0:T(1,128)}), f32[16,1,2560]{2,1,0:T(1,128)S(1)}, u32[]{:S(2)}, u32[]{:S(2)}) async-start(f32[16,1,2560]{2,1,0:T(1,128)} %reshape.475), calls=%async_computation.2 | async-start | bytes 327680 | tf_op jit(solution)/shard_map/all_to_all | solution.py:187
  148.2 12.6 %while.22 = (s32[]{:T(128)}, f32[64,64]{1,0:T(8,128)S(1)}, s32[8,32,32]{2,1,0:T(8,128)}, s32[8,32,32]{2,1,0:T(8,128)}, f32[8,32,32]{2,1,0:T(8,128)S(1)}, /*index=5*/s32[]{:T(128)}, s32[]{:T(128)}) while((s32[]{:T(128)}, f32[64,64]{1,0:T(8,128)S(1)}, s32[8,32,32]{2,1,0:T(8,128)}, s32[8,32,32]{2,1,0:T(8,128)}, ...), condition=%wide.region_4.5_spmd.clone.clone, body=%wide.region_3.4_spmd.clone.clone.sunk | while | flops 50536448 | bytes 94311 | solution.py:113
  160.8 40.8 %psum.15 = f32[64,64]{1,0:T(8,128)S(1)} all-reduce(f32[64,64]{1,0:T(8,128)S(1)} %get-tuple-element.157), channel_id=1, replica_groups=mesh['gx'=16,'gy'=2] {'gx','gy'}, use_global_device_ids=true, to_apply=%region_5.6 | all-reduce | flops 4096 | bytes 32768 | tf_op jit(solution)/shard_map/psum | solution.py:190
  (152 shorter events, 32.4 us)
Async XLA Ops:
  0.6 142.2 %copy-start = (f32[1,128,128]{2,1,0:T(8,128)S(1)}, f32[1,128,128]{2,1,0:T(8,128)}, u32[]{:S(2)}) copy-start(f32[1,128,128]{2,1,0:T(8,128)} %param.40) | copy-start | bytes 196612
  0.6 85.3 %copy-start.1 = (f32[3,8,32,32]{3,2,1,0:T(8,128)S(1)}, f32[3,8,32,32]{3,2,1,0:T(8,128)}, u32[]{:S(2)}) copy-start(f32[3,8,32,32]{3,2,1,0:T(8,128)} %param.34) | copy-start | bytes 294916
  1.6 85.6 %collective-permute-start.1 = (f32[5,1,32,32]{3,2,0,1:T(8,128)S(1)}, f32[5,1,32,32]{3,2,0,1:T(8,128)S(1)}, u32[]{:S(2)}, u32[]{:S(2)}) collective-permute-start(f32[5,1,32,32]{3,2,0,1:T(8,128)S(1)} %get-tuple-element.223), channel_id=1, source_target_pairs={{2,0},{4,2},{6,4},{8,6},{10,8},{12,10},{14,12},{16,14},{18,16},{20... | collective-permute-start | bytes 61448 | tf_op jit(solution)/shard_map/ppermute | solution.py:24
  2.9 84.3 %collective-permute-start = (f32[5,1,32,32]{3,2,0,1:T(8,128)S(1)}, f32[5,1,32,32]{3,2,0,1:T(8,128)S(1)}, u32[]{:S(2)}, u32[]{:S(2)}) collective-permute-start(f32[5,1,32,32]{3,2,0,1:T(8,128)S(1)} %get-tuple-element.222), channel_id=1, source_target_pairs={{0,2},{2,4},{4,6},{6,8},{8,10},{10,12},{12,14},{14,16},{16,18},{18... | collective-permute-start | bytes 61448 | tf_op jit(solution)/shard_map/ppermute | solution.py:23
  8.4 0.7 copy-start.8
  8.4 0.7 copy-start.7
  9.1 0.7 copy-start.4
  9.1 0.7 copy-start.5
  9.9 76.0 %copy-start.3 = (f32[8,32,32]{2,1,0:T(8,128)S(1)}, f32[8,32,32]{2,1,0:T(8,128)}, u32[]{:S(2)}) copy-start(f32[8,32,32]{2,1,0:T(8,128)} %param.33) | copy-start | bytes 98308
  10.1 75.8 %copy-start.2 = (f32[8,32,32]{2,1,0:T(8,128)S(1)}, f32[8,32,32]{2,1,0:T(8,128)}, u32[]{:S(2)}) copy-start(f32[8,32,32]{2,1,0:T(8,128)} %param.35) | copy-start | bytes 98308
  85.9 0.7 copy-start.9
  88.3 6.7 %collective-permute-start.3 = (f32[5,10,32,1]{2,3,1,0:T(1,128)S(1)}, f32[5,10,32,1]{2,3,1,0:T(1,128)S(1)}, u32[]{:S(2)}, u32[]{:S(2)}) collective-permute-start(f32[5,10,32,1]{2,3,1,0:T(1,128)S(1)} %copy.82), channel_id=1, source_target_pairs={{1,0},{3,2},{5,4},{7,6},{9,8},{11,10},{13,12},{15,14},{17,16},{19,... | collective-permute-start | bytes 19208 | tf_op jit(solution)/shard_map/ppermute | solution.py:24
  89.6 5.1 %collective-permute-start.2 = (f32[5,10,32,1]{2,3,1,0:T(1,128)S(1)}, f32[5,10,32,1]{2,3,1,0:T(1,128)S(1)}, u32[]{:S(2)}, u32[]{:S(2)}) collective-permute-start(f32[5,10,32,1]{2,3,1,0:T(1,128)S(1)} %copy.81), channel_id=1, source_target_pairs={{0,1},{2,3},{4,5},{6,7},{8,9},{10,11},{12,13},{14,15},{16,17},{18,... | collective-permute-start | bytes 19208 | tf_op jit(solution)/shard_map/ppermute | solution.py:23
  92.7 0.7 copy-start.6
  117.9 10.9 %all-to-all-start.1 = ((f32[16,1,512]{2,1,0:T(1,128)}), f32[16,1,512]{2,1,0:T(1,128)S(1)}, u32[]{:S(2)}, u32[]{:S(2)}) async-start(f32[16,1,512]{2,1,0:T(1,128)} %reshape.473), calls=%async_computation.1 | async-start | bytes 65536 | tf_op jit(solution)/shard_map/all_to_all | solution.py:183
  128.7 12.8 %all-to-all-start = ((f32[16,1,2560]{2,1,0:T(1,128)}), f32[16,1,2560]{2,1,0:T(1,128)S(1)}, u32[]{:S(2)}, u32[]{:S(2)}) async-start(f32[16,1,2560]{2,1,0:T(1,128)} %reshape.471), calls=%async_computation | async-start | bytes 327680 | tf_op jit(solution)/shard_map/all_to_all | solution.py:180
  144.7 57.5 %all-to-all-start.2 = ((f32[16,1,2560]{2,1,0:T(1,128)}), f32[16,1,2560]{2,1,0:T(1,128)S(1)}, u32[]{:S(2)}, u32[]{:S(2)}) async-start(f32[16,1,2560]{2,1,0:T(1,128)} %reshape.475), calls=%async_computation.2 | async-start | bytes 327680 | tf_op jit(solution)/shard_map/all_to_all | solution.py:187
